TPU v7x, 256 devices: a whole 4x4x8 slice. The times are simulated.
256 devices in a mesh: feat: 32 (over y, z), dp: 8 (over x, core).
Axes of the slice: x: 4, y: 4, z: 8, core: 2. Of those that a mesh axis runs over, the one named last changes fastest.
Arguments:
- query_grads: bfloat16 [512, 131072], P(('dp', 'feat')), may hold values from -52 to 52
- build_grads: bfloat16 [1024, 131072], P('dp', 'feat'), may hold values from -52 to 52
- scored_grads: bfloat16 [4096, 131072], P('dp', 'feat'), may hold values from -52 to 52
Outputs:
- scores: float32 [4096, 512], P(('dp', 'feat'))
All inputs are finite; a program needn't handle non-finite values.
Results may differ from a plain program's by a relative error of at most 0.0049.
Values may be sent and summed in bfloat16 or wider, within the bound.
No kernel may reach another device: no remote copies, remote signals or barrier semaphores. Data moves between devices by JAX's collectives and lax.ppermute only.
A program may use at most 128 MiB of HBM per device.

v0:
```python
import functools
import jax, jax.numpy as jnp
from jax import lax
from jax.experimental import pallas as pl
from jax.experimental.pallas import tpu as pltpu

BLK = 128
FEAT = 131072
BF = jnp.bfloat16
F32 = jnp.float32

def split3(x):
    h = x.astype(BF)
    r = x - h.astype(F32)
    m = r.astype(BF)
    l = (r - m.astype(F32)).astype(BF)
    return h, m, l

def split2(x):
    h = x.astype(BF)
    return h, (x - h.astype(F32)).astype(BF)

def left6(x):
    h, m, l = split3(x)
    return jnp.concatenate([h, h, m, m, h, l], axis=1)

def right6(x):
    h, m, l = split3(x)
    return jnp.concatenate([h, m, h, m, l, h], axis=0)

def left4(x):
    h, m = split2(x)
    return jnp.concatenate([h, h, m, m], axis=1)

def mixed4(x):
    h, m = split2(x)
    return jnp.concatenate([h, m, h, m], axis=1)

def mm(a, b):
    return jnp.dot(a, b, preferred_element_type=F32)

def across(a, b):
    return lax.dot_general(a, b, (((1,), (1,)), ((), ())), preferred_element_type=F32)

def put_rows(x, j, row0, row1):
    g = j // 8 * 8
    sub = lax.broadcasted_iota(jnp.int32, (8, x.shape[1]), 0)
    block = jnp.where(sub == j - g, row0, jnp.where(sub == j - g + 1, row1, x[g:g+8]))
    parts = ([x[:g]] if g else []) + [block] + ([x[g+8:]] if g + 8 < x.shape[0] else [])
    return jnp.concatenate(parts, axis=0)

def sweep(p, off, tick):
    rows = p.shape[0]
    lane = lax.broadcasted_iota(jnp.int32, (1, p.shape[1]), 1)
    def spread(x, i):
        return jnp.broadcast_to(x[:, i:i+1], x.shape)
    c0, c1 = spread(p, off), spread(p, off + 1)
    for j in range(0, rows, 2):
        e, f, h = c0[j:j+1], c0[j+1:j+2], c1[j+1:j+2]
        inv = 1.0 / (e * h - f * f)
        i00, i01, i11 = h * inv, -f * inv, e * inv
        more = j + 2 < rows
        if more:
            d0, d1 = spread(p, off + j + 2), spread(p, off + j + 3)
            x0, x1 = c0[j+2:j+3], c1[j+2:j+3]
            y0, y1 = c0[j+3:j+4], c1[j+3:j+4]
            u0, u1 = i00 * x0 + i01 * x1, i01 * x0 + i11 * x1
            v0, v1 = i00 * y0 + i01 * y1, i01 * y0 + i11 * y1
            n0 = put_rows(d0 - c0 * u0 - c1 * u1, j, u0, u1)
            n1 = put_rows(d1 - c0 * v0 - c1 * v1, j, v0, v1)
        first, second = lane == off + j, lane == off + j + 1
        r0 = jnp.where(first, 1.0, jnp.where(second, 0.0, p[j:j+1]))
        r1 = jnp.where(first, 0.0, jnp.where(second, 1.0, p[j+1:j+2]))
        t0 = i00 * r0 + i01 * r1
        t1 = i01 * r0 + i11 * r1
        p = put_rows(jnp.where(first | second, 0.0, p) - c0 * t0 - c1 * t1, j, t0, t1)
        if more:
            c0, c1 = n0, n1
        tick()
    return p

def inverse(a, tick):
    n = a.shape[0]
    h = n // 2
    left = lax.broadcasted_iota(jnp.int32, (1, n), 1) < h
    top = sweep(a[:h], 0, tick)
    low = jnp.where(left, 0.0, a[h:]) - mm(left6(a[h:, :h]), right6(top))
    low = sweep(low, h, tick)
    high = jnp.where(left, top, 0.0) - mm(left6(top[:, h:]), right6(low))
    return jnp.concatenate([high, low], axis=0)

TILE = 256

class Spread:
    def __init__(self, tasks, steps):
        self.tasks, self.steps, self.step, self.done = tasks, steps, 0, 0
    def __call__(self):
        self.step += 1
        upto = len(self.tasks) * self.step // self.steps
        while self.done < upto:
            self.tasks[self.done]()
            self.done += 1

def solve_kernel(n, nq, place_ref, *refs):
    pieces, (sb_ref, sq_ref, out_ref, a, t, z, s, dinv, w, la, lt, lz, dq) = refs[:7], refs[7:]
    g = n // BLK
    ns = sb_ref.shape[0]
    qs = nq // g
    rows = BLK + qs
    tiles = n // TILE
    chip, core = place_ref[0], place_ref[1]
    chips = n // 256
    own, mate, right, left, side_mates, far, far_mate = pieces
    whole = chips * rows
    places = [(own, 0), (mate, 0), (right, 0), (side_mates, 0), (far, 0), (far_mate, 0), (left, 0), (side_mates, whole)]
    for dx in range(chips):
        there = lax.rem(chip + dx, chips)
        sc = pl.ds(pl.multiple_of(there * 2 * qs, 2 * qs), 2 * qs)
        zc = pl.ds(pl.multiple_of(there * 256, 256), 256)
        def score_rows(i, _, dx=dx, sc=sc, zc=zc):
            r = pl.ds(pl.multiple_of(i * 64, 64), 64)
            s[r, sc] = sq_ref[r, dx*2*qs:(dx+1)*2*qs]
            z[r, zc] = sb_ref[r, dx*256:(dx+1)*256]
            return 0
        lax.fori_loop(0, ns // 64, score_rows, 0)
        for flip in range(2):
            k = there * 2 + lax.rem(core + flip, 2)
            ks = pl.ds(pl.multiple_of(k * BLK, BLK), BLK)
            ts = pl.ds(pl.multiple_of(k * qs, qs), qs)
            ref, r0 = places[dx * 2 + flip]
            def columns(c, _, ref=ref, r0=r0, ks=ks, ts=ts):
                cs = pl.ds(pl.multiple_of(c * 256, 256), 256)
                a[ks, cs] = ref[pl.ds(pl.multiple_of(r0 + c * rows, 8), BLK), :]
                t[ts, cs] = ref[pl.ds(pl.multiple_of(r0 + c * rows + BLK, 8), qs), :]
                return 0
            lax.fori_loop(0, chips, columns, 0)
    tot = jnp.zeros((BLK, BLK), F32)
    eye = (lax.broadcasted_iota(jnp.int32, (BLK, BLK), 0) == lax.broadcasted_iota(jnp.int32, (BLK, BLK), 1)).astype(F32)
    blocks = [slice(k*BLK, (k+1)*BLK) for k in range(g)]
    squares = []
    for k in range(g):
        after = blocks[(k + 1) % g]
        squares.append(a[k*BLK:k*BLK+1, after][:, :qs])
        a[blocks[k], after] = jnp.transpose(a[after, blocks[k]])
        tot = tot + a[blocks[k], blocks[k]] * eye
    per = 256 // qs
    squares = [jnp.concatenate(squares[h*per:(h+1)*per], axis=1) for h in range(nq // 256)]
    trace = jnp.sum(jnp.sum(tot, axis=1, keepdims=True), axis=0, keepdims=True)
    damping = 0.1 * trace / (n * FEAT) + 1e-06
    for d in blocks:
        a[d, d] = a[d, d] + eye * (n * damping)
    dq[...] = jnp.zeros(dq.shape, F32)

    def strip(i):
        return slice(i * TILE, (i + 1) * TILE)

    def score_tasks(ks, d):
        d4 = right6(d)[:4*BLK]
        def dots(rt):
            r = strip(rt)
            lt[r, :] = left4(t[r, ks])
            dq[r, :] = dq[r, :] + mm(lt[r, :], d4) * t[r, ks]
        def scores(rt):
            r = strip(rt)
            lz[r, :] = left4(z[r, ks])
            v = mixed4(mm(lz[r, :], d4))
            for ct in range(nq // TILE):
                c = strip(ct)
                s[r, c] = s[r, c] - across(v, lt[c, :])
        return [functools.partial(dots, i) for i in range(nq // TILE)] + [functools.partial(scores, i) for i in range(ns // TILE)]

    def forward(lo, k, _):
        ks = pl.ds(pl.multiple_of(lax.rem(k + g - 1, g) * BLK, BLK), BLK)
        ns_ = pl.ds(pl.multiple_of(k * BLK, BLK), BLK)
        d = dinv[...]
        dl = left6(d)
        near = mm(dl, right6(a[ks, ns_]))
        block = a[ns_, ns_] - mm(left6(a[ns_, ks]), right6(near))

        def make_w(ct):
            c = strip(ct)
            cc = lax.broadcasted_iota(jnp.int32, (1, TILE), 1) + ct * TILE
            w[:, c] = right6(jnp.where(cc >= k * BLK, mm(dl, right6(a[ks, c])), 0.0))
        def make_la(rt):
            la[strip(rt), :] = left6(a[strip(rt), ks])
        def update(ref, left, terms, rt, ct):
            r, c = strip(rt), strip(ct)
            ref[r, c] = ref[r, c] - mm(left[r, :], w[:terms*BLK, c])
        tasks = [functools.partial(make_w, i) for i in range(lo, tiles)]
        tasks += [functools.partial(make_la, i) for i in range(lo, tiles)]
        tasks += score_tasks(ks, d)
        for ct in range(lo, tiles):
            tasks += [functools.partial(update, a, la, 6, rt, ct) for rt in range(lo, tiles)]
            tasks += [functools.partial(update, t, lt, 4, rt, ct) for rt in range(nq // TILE)]
            tasks += [functools.partial(update, z, lz, 4, rt, ct) for rt in range(ns // TILE)]
        tick = Spread(tasks, BLK // 2)
        dinv[...] = inverse(block, tick)
        return 0

    dinv[...] = jnp.zeros(dinv.shape, F32)
    for first, last, lo in SECTIONS:
        lax.fori_loop(first, last, functools.partial(forward, lo), 0)
    for task in score_tasks(slice(n - BLK, n), dinv[...]):
        task()

    ones = jnp.ones((8, 3 * BLK), BF)
    for h in range(nq // 256):
        c = strip(h)
        dots = across(ones, jnp.concatenate(split3(dq[c, :]), axis=1))[:1]
        self_score = (squares[h] - dots) / damping
        out_ref[:, c] = (s[:, c] * (1.0 / (damping * jnp.sqrt(self_score)))).astype(BF)

SECTIONS = ((0, 5, 0), (5, 8, 2))

def products_kernel(scored_ref, *refs):
    rows_refs, out_ref = refs[:-1], refs[-1]
    @pl.when(pl.program_id(0) == 0)
    def _():
        out_ref[...] = jnp.zeros(out_ref.shape, F32)
    def body(i, _):
        r = pl.ds(pl.multiple_of(i * 256, 256), 256)
        x = scored_ref[r, :]
        for j in range(out_ref.shape[1] // 256):
            each = len(rows_refs) * 256 // out_ref.shape[1]
            c = slice(j * 256, (j + 1) * 256)
            block = jnp.concatenate([ref[...] for ref in rows_refs[j*each:(j+1)*each]], axis=0)
            out_ref[r, c] = out_ref[r, c] + across(x, block)
        return 0
    lax.fori_loop(0, scored_ref.shape[0] // 256, body, 0)

def products(scored, groups):
    ns, width = scored.shape
    n = sum(x.shape[0] for x in groups)
    step = 1024
    cut = lambda x: pl.BlockSpec((x.shape[0], step), lambda i: (0, i))
    return pl.pallas_call(
        products_kernel,
        grid=(width // step,),
        out_shape=jax.ShapeDtypeStruct((ns, n), F32),
        in_specs=[cut(x) for x in (scored, *groups)],
        out_specs=pl.BlockSpec((ns, n), lambda i: (0, 0)),
        compiler_params=pltpu.CompilerParams(vmem_limit_bytes=32 * 1024 * 1024),
        cost_estimate=pl.CostEstimate(flops=2 * ns * width * n, bytes_accessed=2 * width * (ns + n), transcendentals=0),
        name="products",
    )(scored, *groups)

def solve(place, pieces, sb, sq):
    ns, n = sb.shape
    nq = sq.shape[1]
    vm = pl.BlockSpec(memory_space=pltpu.VMEM)
    return pl.pallas_call(
        functools.partial(solve_kernel, n, nq),
        out_shape=jax.ShapeDtypeStruct((ns, nq), BF),
        in_specs=[pl.BlockSpec(memory_space=pltpu.SMEM)] + [vm] * 9, out_specs=vm,
        scratch_shapes=[pltpu.VMEM((n, n), F32), pltpu.VMEM((nq, n), F32), pltpu.VMEM((ns, n), F32), pltpu.VMEM((ns, nq), F32),
                        pltpu.VMEM((BLK, BLK), F32), pltpu.VMEM((6*BLK, n), BF), pltpu.VMEM((n, 6*BLK), BF),
                        pltpu.VMEM((nq, 4*BLK), BF), pltpu.VMEM((ns, 4*BLK), BF), pltpu.VMEM((nq, BLK), F32)],
        compiler_params=pltpu.CompilerParams(vmem_limit_bytes=48 * 1024 * 1024),
        cost_estimate=pl.CostEstimate(flops=20_000_000_000, bytes_accessed=12_000_000, transcendentals=0),
        name="solve",
    )(place, *pieces, sb, sq)


from jax.sharding import Mesh
from jax.sharding import PartitionSpec as P

FEAT_AXES = ("feat_0", "feat_1")
DP = ("dp_0", "dp_1")
DP_FEAT = ("dp_0", "dp_1", "feat_0", "feat_1")


def exchange(x):
    return lax.all_to_all(x, FEAT_AXES, 0, 0, tiled=True)


def shift(x, by):
    size = lax.axis_size("dp_0")
    return lax.ppermute(x, "dp_0", [(i, (i + by) % size) for i in range(size)])


def swap(x):
    return lax.ppermute(x, "dp_1", [(0, 1), (1, 0)])


def beside(x):
    return shift(x, 1), shift(x, -1)


def beyond(left, right):
    half = left.shape[0] // 2
    return jnp.concatenate([shift(left[:half], 1), shift(right[half:], -1)], axis=0)


def paired(parts, core):
    x, mate, right, left, side_mates, far, far_mate = parts
    swapped, count = core != 0, x.shape[0]
    pairs = []
    for one, two in ((x, mate), (right, side_mates[:count]), (far, far_mate), (left, side_mates[count:])):
        pairs += [jnp.where(swapped, two, one), jnp.where(swapped, one, two)]
    return pairs


def on_device(query_grads, build_grads, scored_grads):
    chip, core = lax.axis_index("dp_0"), lax.axis_index("dp_1")
    chips = lax.axis_size("dp_0")
    place = jnp.stack([chip, core]).astype(jnp.int32)
    size = lax.axis_size(FEAT_AXES)
    mate = swap(build_grads)
    left, right = beside(build_grads)
    q_local = lax.all_to_all(query_grads, FEAT_AXES, split_axis=1, concat_axis=0, tiled=True)
    left, right, q_local = lax.optimization_barrier((left, right, q_local))
    far = beyond(left, right)
    sides = swap(jnp.concatenate([right, left], axis=0))
    build_parts = [build_grads, mate, right, left, sides, far, swap(far)]
    query_wide = q_local.astype(F32)
    squares = jnp.sum(query_wide * query_wide, axis=1)
    rows = jnp.concatenate([build_grads, q_local], axis=0)
    build_pairs = paired(build_parts, core)
    sums = jnp.zeros((chips, rows.shape[0], 2 * BLK), F32)
    for i in range(chips):
        pair = jnp.concatenate(build_pairs[2 * i:2 * i + 2], axis=0)
        sums = lax.dynamic_update_slice(sums, across(rows, pair)[None], ((chip + i) % chips, 0, 0))
    after = (chip * 2 + core + 1) % (2 * chips)
    sums = lax.dynamic_update_slice(sums, squares[None, None], (after // 2, 0, after % 2 * BLK))
    q_local, sums = lax.optimization_barrier((q_local, sums))
    q_left, q_right = beside(q_local)
    sums = jnp.sum(exchange(sums.reshape(size, -1, 2 * BLK)), axis=0)
    sums, q_left, q_right = lax.optimization_barrier((sums, q_left, q_right))
    q_far = shift(q_left, 1)
    sums = exchange(jnp.broadcast_to(sums[None], (size, *sums.shape))).reshape(-1, 2 * BLK)
    straight = jnp.concatenate([q_local, q_right, q_far, q_left], axis=0)
    sums, straight, scored_grads = lax.optimization_barrier((sums, straight, scored_grads))
    left, right = beside(sums)
    mate = swap(sums)
    crossed = swap(straight)
    score_build = products(scored_grads, build_pairs)
    left, right, crossed, score_build = lax.optimization_barrier((left, right, crossed, score_build))
    far = beyond(left, right)
    sides = swap(jnp.concatenate([right, left], axis=0))
    blocks = lambda x: x.reshape(chips, -1, x.shape[1])
    first = jnp.where(core == 0, straight, crossed)
    second = jnp.where(core == 0, crossed, straight)
    query_all = jnp.concatenate([blocks(first), blocks(second)], axis=1).reshape(2, -1, first.shape[1])
    score_query = products(scored_grads, [query_all[0], query_all[1]])
    far, score_query = lax.optimization_barrier((far, score_query))
    partial_value = solve(place, [sums, mate, right, left, sides, far, swap(far)], score_build, score_query)
    partial_value = exchange(partial_value.reshape(size, -1, partial_value.shape[1]))
    return jnp.sum(partial_value.astype(F32), axis=0)


def solution(mesh):
    torus = Mesh(mesh.devices.reshape(4, 8, 4, 2), ("feat_0", "feat_1", "dp_0", "dp_1"))
    in_specs = (P(DP_FEAT, None), P(DP, FEAT_AXES), P(DP, FEAT_AXES))
    out_specs = P(DP_FEAT, None)
    return jax.shard_map(
        on_device, mesh=torus, in_specs=in_specs, out_specs=out_specs, check_vma=False
    )
```

profile of v0, /device:TPU:32, one launch (start us, length us, event | category | flops | bytes accessed | tf_op | source)
XLA Modules:
  0.0 224.2 jit_solution(2500108949739046727)
XLA Ops:
  0.0 1.5 collective-permute-start
  1.5 1.7 collective-permute-start.1
  3.2 28.4 %all_to_all.34 = bf16[2,32,4096]{2,0,1:T(2,128)(2,1)S(1)} all-to-all(bf16[2,32,4096]{2,0,1:T(2,128)(2,1)} %bitcast.42), channel_id=1, replica_groups=mesh['feat_0'=4,'feat_1'=8,'dp_0'=4,'dp_1'=2] {'feat_0','feat_1'}, dimensions={1} | all-to-all | bytes 1048576 | tf_op jit(solution)/shard_map/all_to_all | solution.py:310
  31.7 0.2 all_to_all.26
  31.9 0.9 slice.27
  32.8 0.3 collective-permute-start.4
  33.1 3.0 %collective-permute-start.5 = (bf16[64,4096]{1,0:T(8,128)(2,1)S(1)}, bf16[64,4096]{1,0:T(8,128)(2,1)S(1)}, u32[]{:S(2)}, u32[]{:S(2)}) collective-permute-start(bf16[64,4096]{1,0:T(8,128)(2,1)S(1)} %slice.28), channel_id=1, source_target_pairs={{0,6},{2,0},{4,2},{6,4},{1,7},{3,1},{5,3},{7,5},{8,14},{10,8},{12,... | collective-permute-start | bytes 1572872 | tf_op jit(solution)/shard_map/ppermute | solution.py:278
  36.2 0.1 pad_maximum_fusion.1
  36.3 0.0 copy-start.20
  36.3 0.3 collective-permute-start.3
  36.6 8.9 %collective-permute-done.4 = bf16[64,4096]{1,0:T(8,128)(2,1)S(1)} collective-permute-done((bf16[64,4096]{1,0:T(8,128)(2,1)}, bf16[64,4096]{1,0:T(8,128)(2,1)S(1)}, u32[]{:S(2)}, u32[]{:S(2)}) %collective-permute-start.4) | collective-permute-done | bytes 524320 | tf_op jit(solution)/shard_map/ppermute | solution.py:278
  45.5 2.5 %collective-permute-done.5 = bf16[64,4096]{1,0:T(8,128)(2,1)S(1)} collective-permute-done((bf16[64,4096]{1,0:T(8,128)(2,1)S(1)}, bf16[64,4096]{1,0:T(8,128)(2,1)S(1)}, u32[]{:S(2)}, u32[]{:S(2)}) %collective-permute-start.5) | collective-permute-done | bytes 524320 | tf_op jit(solution)/shard_map/ppermute | solution.py:278
  48.0 0.1 collective-permute-start.6
  48.1 0.0 collective-permute-done.2
  48.2 1.7 broadcast_select_fusion.9
  49.9 0.2 multiply_reduce_fusion
  50.2 1.2 broadcast_in_dim.24
  51.4 1.5 fusion.38
  52.9 0.1 broadcast_select_fusion.5
  53.1 1.4 copy-done.19
  54.5 0.3 broadcast_select_fusion.3
  54.8 2.0 fusion.32
  56.8 1.5 fusion.26
  58.4 1.5 fusion.20
  59.9 1.2 dynamic_update_slice.19
  61.1 6.5 %all-to-all-start.1 = ((f32[32,24,256]{2,1,0:T(8,128)}), f32[32,24,256]{2,1,0:T(8,128)S(1)}, u32[]{:S(2)}, u32[]{:S(2)}) async-start(f32[32,24,256]{2,1,0:T(8,128)} %bitcast.9), calls=%async_computation.1 | async-start | bytes 1572864 | tf_op jit(solution)/shard_map/all_to_all | solution.py:273
  67.7 1.3 collective-permute-start.7
  69.0 2.0 collective-permute-start.8
  71.0 20.0 %all-to-all-done.1 = f32[32,24,256]{2,1,0:T(8,128)S(1)} async-done(((f32[32,24,256]{2,1,0:T(8,128)}), f32[32,24,256]{2,1,0:T(8,128)S(1)}, u32[]{:S(2)}, u32[]{:S(2)}) %all-to-all-start.1) | async-done | bytes 786464 | tf_op jit(solution)/shard_map/all_to_all | solution.py:273
  91.0 0.1 reduce_sum.28
  91.1 0.9 broadcast_in_dim.30
  92.0 5.4 %all-to-all-start.2 = ((f32[32,24,256]{2,1,0:T(8,128)}), f32[32,24,256]{2,1,0:T(8,128)S(1)}, u32[]{:S(2)}, u32[]{:S(2)}) async-start(f32[32,24,256]{2,1,0:T(8,128)} %broadcast_in_dim.30), calls=%async_computation.2 | async-start | bytes 1572864 | tf_op jit(solution)/shard_map/all_to_all | solution.py:273
  97.5 1.3 collective-permute-start.9
  98.8 12.7 %collective-permute-done.9 = bf16[64,4096]{1,0:T(8,128)(2,1)S(1)} collective-permute-done((bf16[64,4096]{1,0:T(8,128)(2,1)S(1)}, bf16[64,4096]{1,0:T(8,128)(2,1)S(1)}, u32[]{:S(2)}, u32[]{:S(2)}) %collective-permute-start.9) | collective-permute-done | bytes 524320 | tf_op jit(solution)/shard_map/ppermute | solution.py:278
  111.5 1.5 pad_maximum_fusion.2
  113.0 7.2 %all-to-all-done.2 = f32[32,24,256]{2,1,0:T(8,128)S(1)} async-done(((f32[32,24,256]{2,1,0:T(8,128)}), f32[32,24,256]{2,1,0:T(8,128)S(1)}, u32[]{:S(2)}, u32[]{:S(2)}) %all-to-all-start.2) | async-done | bytes 786464 | tf_op jit(solution)/shard_map/all_to_all | solution.py:273
  120.2 1.2 collective-permute-start.11
  121.5 2.0 collective-permute-start.12
  123.5 2.2 copy-done
  125.7 1.2 copy-done.2
  126.9 1.2 copy-done.4
  128.1 1.2 copy-done.6
  129.4 1.2 copy-done.8
  130.6 1.2 copy-done.10
  131.8 1.2 copy-done.13
  133.0 1.2 copy-done.15
  134.2 7.0 %products.2.refs_7_ = f32[512,1024]{1,0:T(8,128)S(1)} custom-call(bf16[512,4096]{1,0:T(8,128)(2,1)S(1)} %copy-done, bf16[128,4096]{1,0:T(8,128)(2,1)S(1)} %copy-done.13, bf16[128,4096]{1,0:T(8,128)(2,1)S(1)} %copy-done.15, bf16[128,4096]{1,0:T(8,128)(2,1)S(1)} %copy-done.10, bf16[128,4096]{1,0:T(8,128)(2,1)S(1)} %copy-done.8, ...), custom_call_target="tpu_custom_call" | custom-call | flops 4294967296 | bytes 12582912 | tf_op jit(solution)/shard_map/products/pallas_call | solution.py:236
  141.3 0.1 collective-permute-done.11.refs_3_
  141.5 0.1 pad_maximum_fusion.3
  141.6 1.1 copy-done.16
  142.7 0.4 collective-permute-start.15
  143.1 2.8 %collective-permute-start.16 = (f32[384,256]{1,0:T(8,128)S(1)}, f32[384,256]{1,0:T(8,128)S(1)}, u32[]{:S(2)}, u32[]{:S(2)}) collective-permute-start(f32[384,256]{1,0:T(8,128)S(1)} %slice.31), channel_id=1, source_target_pairs={{0,6},{2,0},{4,2},{6,4},{1,7},{3,1},{5,3},{7,5},{8,14},{10,8},{12,... | collective-permute-start | bytes 1179656 | tf_op jit(solution)/shard_map/ppermute | solution.py:278
  145.9 1.9 broadcast_select_fusion
  147.8 0.5 pad_maximum_fusion
  148.3 4.5 %products.3.refs_8_ = f32[512,512]{1,0:T(8,128)S(1)} custom-call(bf16[512,4096]{1,0:T(8,128)(2,1)S(1)} %copy-done, bf16[256,4096]{1,0:T(8,128)(2,1)S(1)} %bitcast.33, bf16[256,4096]{1,0:T(8,128)(2,1)S(1)} %bitcast.32), custom_call_target="tpu_custom_call" | custom-call | flops 2147483648 | bytes 8388608 | tf_op jit(solution)/shard_map/products/pallas_call | solution.py:236
  152.8 1.0 copy-done.11
  153.8 1.6 collective-permute-done.15
  155.4 0.1 pad_maximum_fusion.4.refs_5_
  155.5 0.3 collective-permute-start.17
  155.8 0.1 pad_add_fusion.place_ref
  155.9 2.2 collective-permute-done.17.refs_6_
  158.1 42.8 %solve.1 = bf16[512,512]{1,0:T(8,128)(2,1)S(1)} custom-call(s32[2]{0:T(128)S(1)} %pad_add_fusion.place_ref, f32[768,256]{1,0:T(8,128)S(1)} %bitcast.37, f32[768,256]{1,0:T(8,128)S(1)} %collective-permute-done.10.refs_1_, f32[768,256]{1,0:T(8,128)S(1)} %collective-permute-done.12.refs_2_, f32[768,256]{1,0:T(8,128)S(1)} %collective-permute-done.11.refs_3_, ...), custom_call_target="tpu_custom_call" | custom-call | flops 20000000000 | bytes 12000000 | tf_op jit(solution)/shard_map/solve/pallas_call | solution.py:251
  200.9 22.7 %all_to_all.35 = bf16[32,16,512]{2,1,0:T(8,128)(2,1)S(1)} all-to-all(bf16[32,16,512]{2,1,0:T(8,128)(2,1)S(1)} %bitcast.38), channel_id=1, replica_groups=mesh['feat_0'=4,'feat_1'=8,'dp_0'=4,'dp_1'=2] {'feat_0','feat_1'}, dimensions={0} | all-to-all | bytes 1048576 | tf_op jit(solution)/shard_map/all_to_all | solution.py:273
  223.5 0.7 convert_reduce_fusion
  (51 shorter events, 0.3 us)
Async XLA Ops:
  0.0 31.9 %collective-permute-start = (bf16[128,4096]{1,0:T(8,128)(2,1)}, bf16[128,4096]{1,0:T(8,128)(2,1)S(1)}, u32[]{:S(2)}, u32[]{:S(2)}) collective-permute-start(bf16[128,4096]{1,0:T(8,128)(2,1)} %param.4), channel_id=1, source_target_pairs={{0,2},{2,4},{4,6},{6,0},{1,3},{3,5},{5,7},{7,1},{8,10},{10,12},{12... | collective-permute-start | bytes 3145736 | tf_op jit(solution)/shard_map/ppermute | solution.py:278
  1.5 30.4 %collective-permute-start.1 = (bf16[128,4096]{1,0:T(8,128)(2,1)}, bf16[128,4096]{1,0:T(8,128)(2,1)S(1)}, u32[]{:S(2)}, u32[]{:S(2)}) collective-permute-start(bf16[128,4096]{1,0:T(8,128)(2,1)} %param.4), channel_id=1, source_target_pairs={{0,6},{2,0},{4,2},{6,4},{1,7},{3,1},{5,3},{7,5},{8,14},{10,8},{12,... | collective-permute-start | bytes 3145736 | tf_op jit(solution)/shard_map/ppermute | solution.py:278
  31.9 4.4 %copy-start.18 = (bf16[128,4096]{1,0:T(8,128)(2,1)}, bf16[128,4096]{1,0:T(8,128)(2,1)S(1)}, u32[]{:S(2)}) copy-start(bf16[128,4096]{1,0:T(8,128)(2,1)S(1)} %collective-permute-done.1) | copy-start | bytes 3145732
  32.8 12.7 %collective-permute-start.4 = (bf16[64,4096]{1,0:T(8,128)(2,1)}, bf16[64,4096]{1,0:T(8,128)(2,1)S(1)}, u32[]{:S(2)}, u32[]{:S(2)}) collective-permute-start(bf16[64,4096]{1,0:T(8,128)(2,1)} %slice.27), channel_id=1, source_target_pairs={{0,2},{2,4},{4,6},{6,0},{1,3},{3,5},{5,7},{7,1},{8,10},{10,12},{12... | collective-permute-start | bytes 1572872 | tf_op jit(solution)/shard_map/ppermute | solution.py:278
  33.1 15.1 %collective-permute-start.2 = (bf16[128,4096]{1,0:T(8,128)(2,1)}, bf16[128,4096]{1,0:T(8,128)(2,1)}, u32[]{:S(2)}, u32[]{:S(2)}) collective-permute-start(bf16[128,4096]{1,0:T(8,128)(2,1)} %param.4), channel_id=1, source_target_pairs={{0,1},{1,0},{2,3},{3,2},{4,5},{5,4},{6,7},{7,6},{8,9},{9,8},{10,11... | collective-permute-start | bytes 3145736 | tf_op jit(solution)/shard_map/ppermute | solution.py:282
  33.1 14.9 %collective-permute-start.5 = (bf16[64,4096]{1,0:T(8,128)(2,1)S(1)}, bf16[64,4096]{1,0:T(8,128)(2,1)S(1)}, u32[]{:S(2)}, u32[]{:S(2)}) collective-permute-start(bf16[64,4096]{1,0:T(8,128)(2,1)S(1)} %slice.28), channel_id=1, source_target_pairs={{0,6},{2,0},{4,2},{6,4},{1,7},{3,1},{5,3},{7,5},{8,14},{10,8},{12,... | collective-permute-start | bytes 1572872 | tf_op jit(solution)/shard_map/ppermute | solution.py:278
  36.3 11.9 %copy-start.20 = (bf16[128,4096]{1,0:T(8,128)(2,1)S(1)}, bf16[128,4096]{1,0:T(8,128)(2,1)}, u32[]{:S(2)}) copy-start(bf16[128,4096]{1,0:T(8,128)(2,1)} %param.4) | copy-start | bytes 3145732
  36.3 16.8 %collective-permute-start.3 = (bf16[256,4096]{1,0:T(8,128)(2,1)S(1)}, bf16[256,4096]{1,0:T(8,128)(2,1)S(1)}, u32[]{:S(2)}, u32[]{:S(2)}) collective-permute-start(bf16[256,4096]{1,0:T(8,128)(2,1)S(1)} %pad_maximum_fusion.1), channel_id=1, source_target_pairs={{0,1},{1,0},{2,3},{3,2},{4,5},{5,4},{6,7},{7,6},{8,9},{9,8},{10,11... | collective-permute-start | bytes 6291464 | tf_op jit(solution)/shard_map/ppermute | solution.py:282
  48.0 4.9 %collective-permute-start.6 = (bf16[128,4096]{1,0:T(8,128)(2,1)S(1)}, bf16[128,4096]{1,0:T(8,128)(2,1)S(1)}, u32[]{:S(2)}, u32[]{:S(2)}) collective-permute-start(bf16[128,4096]{1,0:T(8,128)(2,1)S(1)} %constant_dynamic-update-slice_fusion.2), channel_id=1, source_target_pairs={{0,1},{1,0},{2,3},{3,2},{4,5},{5,4},{6,7},{7,6},{8,9},{9,8},{10,11... | collective-permute-start | bytes 3145736 | tf_op jit(solution)/shard_map/ppermute | solution.py:282
  49.9 3.0 %copy-start.12 = (bf16[128,4096]{1,0:T(8,128)(2,1)}, bf16[128,4096]{1,0:T(8,128)(2,1)S(1)}, u32[]{:S(2)}) copy-start(bf16[128,4096]{1,0:T(8,128)(2,1)S(1)} %get-tuple-element.51.refs_0_) | copy-start | bytes 3145732
  49.9 3.0 %copy-start.14 = (bf16[128,4096]{1,0:T(8,128)(2,1)}, bf16[128,4096]{1,0:T(8,128)(2,1)S(1)}, u32[]{:S(2)}) copy-start(bf16[128,4096]{1,0:T(8,128)(2,1)S(1)} %get-tuple-element.52.refs_1_) | copy-start | bytes 3145732
  52.9 1.6 copy-start.19
  53.1 3.7 %copy-start.1 = (bf16[128,4096]{1,0:T(8,128)(2,1)}, bf16[128,4096]{1,0:T(8,128)(2,1)S(1)}, u32[]{:S(2)}) copy-start(bf16[128,4096]{1,0:T(8,128)(2,1)S(1)} %get-tuple-element.50.refs_5_) | copy-start | bytes 3145732
  54.8 2.0 copy-start.7
  54.8 2.0 copy-start.9
  54.8 3.6 %copy-start.3 = (bf16[128,4096]{1,0:T(8,128)(2,1)}, bf16[128,4096]{1,0:T(8,128)(2,1)S(1)}, u32[]{:S(2)}) copy-start(bf16[128,4096]{1,0:T(8,128)(2,1)S(1)} %get-tuple-element.43.refs_6_) | copy-start | bytes 3145732
  54.8 3.6 %copy-start.5 = (bf16[128,4096]{1,0:T(8,128)(2,1)}, bf16[128,4096]{1,0:T(8,128)(2,1)S(1)}, u32[]{:S(2)}) copy-start(bf16[128,4096]{1,0:T(8,128)(2,1)S(1)} %get-tuple-element.44.refs_7_) | copy-start | bytes 3145732
  61.1 29.9 %all-to-all-start.1 = ((f32[32,24,256]{2,1,0:T(8,128)}), f32[32,24,256]{2,1,0:T(8,128)S(1)}, u32[]{:S(2)}, u32[]{:S(2)}) async-start(f32[32,24,256]{2,1,0:T(8,128)} %bitcast.9), calls=%async_computation.1 | async-start | bytes 1572864 | tf_op jit(solution)/shard_map/all_to_all | solution.py:273
  67.7 23.4 %collective-permute-start.7 = (bf16[64,4096]{1,0:T(8,128)(2,1)S(1)}, bf16[64,4096]{1,0:T(8,128)(2,1)S(1)}, u32[]{:S(2)}, u32[]{:S(2)}) collective-permute-start(bf16[64,4096]{1,0:T(8,128)(2,1)S(1)} %all_to_all.26), channel_id=1, source_target_pairs={{0,2},{2,4},{4,6},{6,0},{1,3},{3,5},{5,7},{7,1},{8,10},{10,12},{12... | collective-permute-start | bytes 1572872 | tf_op jit(solution)/shard_map/ppermute | solution.py:278
  69.0 22.1 %collective-permute-start.8 = (bf16[64,4096]{1,0:T(8,128)(2,1)S(1)}, bf16[64,4096]{1,0:T(8,128)(2,1)S(1)}, u32[]{:S(2)}, u32[]{:S(2)}) collective-permute-start(bf16[64,4096]{1,0:T(8,128)(2,1)S(1)} %all_to_all.26), channel_id=1, source_target_pairs={{0,6},{2,0},{4,2},{6,4},{1,7},{3,1},{5,3},{7,5},{8,14},{10,8},{12,... | collective-permute-start | bytes 1572872 | tf_op jit(solution)/shard_map/ppermute | solution.py:278
  92.0 28.2 %all-to-all-start.2 = ((f32[32,24,256]{2,1,0:T(8,128)}), f32[32,24,256]{2,1,0:T(8,128)S(1)}, u32[]{:S(2)}, u32[]{:S(2)}) async-start(f32[32,24,256]{2,1,0:T(8,128)} %broadcast_in_dim.30), calls=%async_computation.2 | async-start | bytes 1572864 | tf_op jit(solution)/shard_map/all_to_all | solution.py:273
  97.5 14.0 %collective-permute-start.9 = (bf16[64,4096]{1,0:T(8,128)(2,1)S(1)}, bf16[64,4096]{1,0:T(8,128)(2,1)S(1)}, u32[]{:S(2)}, u32[]{:S(2)}) collective-permute-start(bf16[64,4096]{1,0:T(8,128)(2,1)S(1)} %collective-permute-done.7), channel_id=1, source_target_pairs={{0,2},{2,4},{4,6},{6,0},{1,3},{3,5},{5,7},{7,1},{8,10},{10,12},{12... | collective-permute-start | bytes 1572872 | tf_op jit(solution)/shard_map/ppermute | solution.py:278
  120.2 21.2 %collective-permute-start.13 = (bf16[256,4096]{1,0:T(8,128)(2,1)}, bf16[256,4096]{1,0:T(8,128)(2,1)}, u32[]{:S(2)}, u32[]{:S(2)}) collective-permute-start(bf16[256,4096]{1,0:T(8,128)(2,1)} %pad_maximum_fusion.2), channel_id=1, source_target_pairs={{0,1},{1,0},{2,3},{3,2},{4,5},{5,4},{6,7},{7,6},{8,9},{9,8},{10,11... | collective-permute-start | bytes 6291464 | tf_op jit(solution)/shard_map/ppermute | solution.py:282
  120.2 21.2 %collective-permute-start.11 = (f32[768,256]{1,0:T(8,128)S(1)}, f32[768,256]{1,0:T(8,128)S(1)}, u32[]{:S(2)}, u32[]{:S(2)}) collective-permute-start(f32[768,256]{1,0:T(8,128)S(1)} %bitcast.34), channel_id=1, source_target_pairs={{0,2},{2,4},{4,6},{6,0},{1,3},{3,5},{5,7},{7,1},{8,10},{10,12},{12... | collective-permute-start | bytes 2359304 | tf_op jit(solution)/shard_map/ppermute | solution.py:278
  121.5 20.0 %collective-permute-start.12 = (f32[768,256]{1,0:T(8,128)S(1)}, f32[768,256]{1,0:T(8,128)S(1)}, u32[]{:S(2)}, u32[]{:S(2)}) collective-permute-start(f32[768,256]{1,0:T(8,128)S(1)} %bitcast.35), channel_id=1, source_target_pairs={{0,6},{2,0},{4,2},{6,4},{1,7},{3,1},{5,3},{7,5},{8,14},{10,8},{12,... | collective-permute-start | bytes 2359304 | tf_op jit(solution)/shard_map/ppermute | solution.py:278
  123.5 32.4 %collective-permute-start.10 = (f32[768,256]{1,0:T(8,128)S(1)}, f32[768,256]{1,0:T(8,128)S(1)}, u32[]{:S(2)}, u32[]{:S(2)}) collective-permute-start(f32[768,256]{1,0:T(8,128)S(1)} %bitcast.36), channel_id=1, source_target_pairs={{0,1},{1,0},{2,3},{3,2},{4,5},{5,4},{6,7},{7,6},{8,9},{9,8},{10,11... | collective-permute-start | bytes 2359304 | tf_op jit(solution)/shard_map/ppermute | solution.py:282
  123.5 2.2 copy-start
  125.7 1.2 copy-start.2
  126.9 1.2 copy-start.4
  128.1 1.2 copy-start.6
  129.3 1.2 copy-start.8
  130.6 1.2 copy-start.10
  131.8 1.2 copy-start.13
  133.0 1.2 copy-start.15
  141.3 1.4 copy-start.16
  141.5 4.5 %copy-start.17 = (bf16[256,4096]{1,0:T(8,128)(2,1)S(1)}, bf16[256,4096]{1,0:T(8,128)(2,1)}, u32[]{:S(2)}) copy-start(bf16[256,4096]{1,0:T(8,128)(2,1)} %pad_maximum_fusion.2) | copy-start | bytes 6291460
  142.7 12.7 %collective-permute-start.15 = (f32[384,256]{1,0:T(8,128)S(1)}, f32[384,256]{1,0:T(8,128)S(1)}, u32[]{:S(2)}, u32[]{:S(2)}) collective-permute-start(f32[384,256]{1,0:T(8,128)S(1)} %slice.30), channel_id=1, source_target_pairs={{0,2},{2,4},{4,6},{6,0},{1,3},{3,5},{5,7},{7,1},{8,10},{10,12},{12... | collective-permute-start | bytes 1179656 | tf_op jit(solution)/shard_map/ppermute | solution.py:278
  143.1 12.3 %collective-permute-start.16 = (f32[384,256]{1,0:T(8,128)S(1)}, f32[384,256]{1,0:T(8,128)S(1)}, u32[]{:S(2)}, u32[]{:S(2)}) collective-permute-start(f32[384,256]{1,0:T(8,128)S(1)} %slice.31), channel_id=1, source_target_pairs={{0,6},{2,0},{4,2},{6,4},{1,7},{3,1},{5,3},{7,5},{8,14},{10,8},{12,... | collective-permute-start | bytes 1179656 | tf_op jit(solution)/shard_map/ppermute | solution.py:278
  145.9 12.2 %collective-permute-start.14 = (f32[1536,256]{1,0:T(8,128)S(1)}, f32[1536,256]{1,0:T(8,128)}, u32[]{:S(2)}, u32[]{:S(2)}) collective-permute-start(f32[1536,256]{1,0:T(8,128)S(1)} %pad_maximum_fusion.3), channel_id=1, source_target_pairs={{0,1},{1,0},{2,3},{3,2},{4,5},{5,4},{6,7},{7,6},{8,9},{9,8},{10,11... | collective-permute-start | bytes 4718600 | tf_op jit(solution)/shard_map/ppermute | solution.py:282
  152.8 1.0 copy-start.11
  155.5 2.6 %collective-permute-start.17 = (f32[768,256]{1,0:T(8,128)S(1)}, f32[768,256]{1,0:T(8,128)S(1)}, u32[]{:S(2)}, u32[]{:S(2)}) collective-permute-start(f32[768,256]{1,0:T(8,128)S(1)} %pad_maximum_fusion.4.refs_5_), channel_id=1, source_target_pairs={{0,1},{1,0},{2,3},{3,2},{4,5},{5,4},{6,7},{7,6},{8,9},{9,8},{10,11... | collective-permute-start | bytes 2359304 | tf_op jit(solution)/shard_map/ppermute | solution.py:282
where the time goes:
time: 225 us; the launch traced here: 224 us
  waiting for transfers between devices  55.3 us (25%)
  Pallas kernels  54.3 us (24%)
  blocking collectives  51.1 us (23%)
  starting transfers between devices  30.3 us (13%)
  local copies, waits for them, and re-layouts  19 us (8%)
  other arithmetic  7.38 us (3%)
  matrix products  6.57 us (3%)
    pallas_call x1, Pallas kernels, solve(): pl.pallas_call(functools.partial(solve_kernel, n, nq), out_shape=jax.Shap...  42.8 us
    all_to_all x1, blocking collectives, on_device(): lax.all_to_all(query_grads, FEAT_AXES, split_axis=1, concat_axis=0, tiled...  28.4 us
    all_to_all x2, waiting for transfers between devices, exchange(): return lax.all_to_all(x, FEAT_AXES, 0, 0, tiled=True)  27.2 us
    ppermute x11, waiting for transfers between devices, shift(): return lax.ppermute(x, 'dp_0', [(i, (i + by) % size) for i in range(size)])  25.8 us
    all_to_all x1, blocking collectives, exchange(): return lax.all_to_all(x, FEAT_AXES, 0, 0, tiled=True)  22.7 us
    ppermute x11, starting transfers between devices, shift(): return lax.ppermute(x, 'dp_0', [(i, (i + by) % size) for i in range(size)])  17.6 us
    unnamed x43, local copies, waits for them, and re-layouts  14.3 us
    all_to_all x2, starting transfers between devices, exchange(): return lax.all_to_all(x, FEAT_AXES, 0, 0, tiled=True)  11.9 us
  transfers between devices with their start and end apart: 20, of which 8 were waited for; matrix products, arithmetic and copies ran while one was open for 4% of the time, Pallas kernels for 5%

commit v1 on v0

--- a/solution.py
+++ b/solution.py
@@ -239,7 +239,7 @@
         out_shape=jax.ShapeDtypeStruct((ns, n), F32),
         in_specs=[cut(x) for x in (scored, *groups)],
         out_specs=pl.BlockSpec((ns, n), lambda i: (0, 0)),
-        compiler_params=pltpu.CompilerParams(vmem_limit_bytes=32 * 1024 * 1024),
+        compiler_params=pltpu.CompilerParams(vmem_limit_bytes=54 * 1024 * 1024),
         cost_estimate=pl.CostEstimate(flops=2 * ns * width * n, bytes_accessed=2 * width * (ns + n), transcendentals=0),
         name="products",
     )(scored, *groups)
@@ -291,13 +291,8 @@
     return jnp.concatenate([shift(left[:half], 1), shift(right[half:], -1)], axis=0)
 
 
-def paired(parts, core):
-    x, mate, right, left, side_mates, far, far_mate = parts
-    swapped, count = core != 0, x.shape[0]
-    pairs = []
-    for one, two in ((x, mate), (right, side_mates[:count]), (far, far_mate), (left, side_mates[count:])):
-        pairs += [jnp.where(swapped, two, one), jnp.where(swapped, one, two)]
-    return pairs
+def ordered(one, two, core):
+    return [jnp.where(core != 0, two, one), jnp.where(core != 0, one, two)]
 
 
 def on_device(query_grads, build_grads, scored_grads):
@@ -309,32 +304,40 @@
     left, right = beside(build_grads)
     q_local = lax.all_to_all(query_grads, FEAT_AXES, split_axis=1, concat_axis=0, tiled=True)
     left, right, q_local = lax.optimization_barrier((left, right, q_local))
+    sides = swap(jnp.concatenate([right, left], axis=0))
     far = beyond(left, right)
-    sides = swap(jnp.concatenate([right, left], axis=0))
-    build_parts = [build_grads, mate, right, left, sides, far, swap(far)]
     query_wide = q_local.astype(F32)
     squares = jnp.sum(query_wide * query_wide, axis=1)
     rows = jnp.concatenate([build_grads, q_local], axis=0)
-    build_pairs = paired(build_parts, core)
+    count = build_grads.shape[0]
+    near = [ordered(build_grads, mate, core), ordered(right, sides[:count], core), ordered(left, sides[count:], core)]
     sums = jnp.zeros((chips, rows.shape[0], 2 * BLK), F32)
-    for i in range(chips):
-        pair = jnp.concatenate(build_pairs[2 * i:2 * i + 2], axis=0)
-        sums = lax.dynamic_update_slice(sums, across(rows, pair)[None], ((chip + i) % chips, 0, 0))
+
+    def placed(sums, pair, step):
+        value = across(rows, jnp.concatenate(pair, axis=0))
+        return lax.dynamic_update_slice(sums, value[None], ((chip + step) % chips, 0, 0))
+
+    for step, pair in zip((0, 1, 3), near):
+        sums = placed(sums, pair, step)
+    far, sums = lax.optimization_barrier((far, sums))
+    distant = ordered(far, swap(far), core)
+    sums = placed(sums, distant, 2)
+    build_pairs = near[0] + near[1] + distant + near[2]
     after = (chip * 2 + core + 1) % (2 * chips)
     sums = lax.dynamic_update_slice(sums, squares[None, None], (after // 2, 0, after % 2 * BLK))
     q_local, sums = lax.optimization_barrier((q_local, sums))
     q_left, q_right = beside(q_local)
     sums = jnp.sum(exchange(sums.reshape(size, -1, 2 * BLK)), axis=0)
-    sums, q_left, q_right = lax.optimization_barrier((sums, q_left, q_right))
+    sums, q_left, q_right, scored_grads = lax.optimization_barrier((sums, q_left, q_right, scored_grads))
     q_far = shift(q_left, 1)
     sums = exchange(jnp.broadcast_to(sums[None], (size, *sums.shape))).reshape(-1, 2 * BLK)
     straight = jnp.concatenate([q_local, q_right, q_far, q_left], axis=0)
-    sums, straight, scored_grads = lax.optimization_barrier((sums, straight, scored_grads))
+    score_build = products(scored_grads, build_pairs)
+    sums, straight, score_build = lax.optimization_barrier((sums, straight, score_build))
     left, right = beside(sums)
     mate = swap(sums)
     crossed = swap(straight)
-    score_build = products(scored_grads, build_pairs)
-    left, right, crossed, score_build = lax.optimization_barrier((left, right, crossed, score_build))
+    left, right, crossed = lax.optimization_barrier((left, right, crossed))
     far = beyond(left, right)
     sides = swap(jnp.concatenate([right, left], axis=0))
     blocks = lambda x: x.reshape(chips, -1, x.shape[1])
@@ -352,6 +355,5 @@
     torus = Mesh(mesh.devices.reshape(4, 8, 4, 2), ("feat_0", "feat_1", "dp_0", "dp_1"))
     in_specs = (P(DP_FEAT, None), P(DP, FEAT_AXES), P(DP, FEAT_AXES))
     out_specs = P(DP_FEAT, None)
-    return jax.shard_map(
-        on_device, mesh=torus, in_specs=in_specs, out_specs=out_specs, check_vma=False
-    )
+
+    return jax.shard_map(on_device, mesh=torus, in_specs=in_specs, out_specs=out_specs, check_vma=False)

time: 225 us -> 225 us (level)
  blocking collectives: 51.1 us -> 22.9 us
  waiting for transfers between devices: 55.3 us -> 77.3 us
  local copies, waits for them, and re-layouts: 19 us -> 3.74 us
  starting transfers between devices: 30.3 us -> 41 us
  other arithmetic: 7.38 us -> 13.1 us
  Pallas kernels: 54.3 us -> 59.7 us
    all_to_all x1 -> x0, blocking collectives: 28.4 us -> none  [on_device(): lax.all_to_all(query_grads, FEAT_AXES, split_axis=1, concat_axis=0, tiled...]
    all_to_all x0 -> x1, waiting for transfers between devices: none -> 16.9 us  [on_device(): lax.all_to_all(query_grads, FEAT_AXES, split_axis=1, concat_axis=0, tiled...]
    unnamed x43 -> x22, local copies, waits for them, and re-layouts: 14.3 us -> 0.05 us
    all_to_all x0 -> x1, starting transfers between devices: none -> 11.4 us  [on_device(): lax.all_to_all(query_grads, FEAT_AXES, split_axis=1, concat_axis=0, tiled...]
    pallas_call x2, Pallas kernels: 11.5 us -> 16.9 us  [products(): pl.pallas_call(products_kernel, grid=(width // step,), out_shape=jax.Shap...]
    ppermute x11, waiting for transfers between devices: 25.8 us -> 28.6 us  [shift(): return lax.ppermute(x, 'dp_0', [(i, (i + by) % size) for i in range(size)])]
    ppermute x7, waiting for transfers between devices: 2.21 us -> 4.5 us  [swap(): return lax.ppermute(x, 'dp_1', [(0, 1), (1, 0)])]
  transfers between devices with their start and end apart: 20 -> 21, of which waited for: 8 -> 8; matrix products, arithmetic and copies ran while one was open for 4% -> 6% of each run, Pallas kernels for 5% -> 8%
where the time goes in v1:
time: 225 us
  waiting for transfers between devices  77.3 us (34%)
  Pallas kernels  59.7 us (27%)
  starting transfers between devices  41 us (18%)
  blocking collectives  22.9 us (10%)
  other arithmetic  13.1 us (6%)
  matrix products  6.65 us (3%)
  local copies, waits for them, and re-layouts  3.74 us (2%)
    pallas_call x1, Pallas kernels, solve(): pl.pallas_call(functools.partial(solve_kernel, n, nq), out_shape=jax.Shap...  42.8 us
    ppermute x11, waiting for transfers between devices, shift(): return lax.ppermute(x, 'dp_0', [(i, (i + by) % size) for i in range(size)])  28.6 us
    all_to_all x2, waiting for transfers between devices, exchange(): return lax.all_to_all(x, FEAT_AXES, 0, 0, tiled=True)  27.3 us
    all_to_all x1, blocking collectives, exchange(): return lax.all_to_all(x, FEAT_AXES, 0, 0, tiled=True)  22.9 us
    ppermute x11, starting transfers between devices, shift(): return lax.ppermute(x, 'dp_0', [(i, (i + by) % size) for i in range(size)])  17.7 us
    all_to_all x1, waiting for transfers between devices, on_device(): lax.all_to_all(query_grads, FEAT_AXES, split_axis=1, concat_axis=0, tiled...  16.9 us
    pallas_call x2, Pallas kernels, products(): pl.pallas_call(products_kernel, grid=(width // step,), out_shape=jax.Shap...  16.9 us
    all_to_all x1, starting transfers between devices, on_device(): lax.all_to_all(query_grads, FEAT_AXES, split_axis=1, concat_axis=0, tiled...  11.4 us
  transfers between devices with their start and end apart: 21, of which 8 were waited for; matrix products, arithmetic and copies ran while one was open for 6% of the time, Pallas kernels for 8%

profile of v1, /device:TPU:32, one launch (start us, length us, event | category | flops | bytes accessed | tf_op | source)
XLA Modules:
  0.0 224.7 jit_solution(2699354820269357006)
XLA Ops:
  0.0 1.5 collective-permute-start
  1.5 1.7 collective-permute-start.1
  3.2 11.4 %all-to-all-start = ((bf16[2,32,4096]{2,0,1:T(2,128)(2,1)}), bf16[2,32,4096]{2,0,1:T(2,128)(2,1)S(1)}, u32[]{:S(2)}, u32[]{:S(2)}) async-start(bf16[2,32,4096]{2,0,1:T(2,128)(2,1)} %bitcast.42), calls=%async_computation | async-start | bytes 1048576 | tf_op jit(solution)/shard_map/all_to_all | solution.py:305
  14.6 0.1 collective-permute-start.4
  14.8 16.9 %all-to-all-done = bf16[2,32,4096]{2,0,1:T(2,128)(2,1)S(1)} async-done(((bf16[2,32,4096]{2,0,1:T(2,128)(2,1)}), bf16[2,32,4096]{2,0,1:T(2,128)(2,1)S(1)}, u32[]{:S(2)}, u32[]{:S(2)}) %all-to-all-start) | async-done | bytes 524320 | tf_op jit(solution)/shard_map/all_to_all | solution.py:305
  31.7 0.2 all_to_all.26
  31.9 0.0 collective-permute-done
  32.0 0.0 copy-start.6
  32.0 0.1 pad_maximum_fusion.1
  32.1 0.1 collective-permute-start.5
  32.2 0.4 collective-permute-start.2
  32.6 3.0 %collective-permute-start.3 = (bf16[64,4096]{1,0:T(8,128)(2,1)S(1)}, bf16[64,4096]{1,0:T(8,128)(2,1)S(1)}, u32[]{:S(2)}, u32[]{:S(2)}) collective-permute-start(bf16[64,4096]{1,0:T(8,128)(2,1)S(1)} %slice.27), channel_id=1, source_target_pairs={{0,6},{2,0},{4,2},{6,4},{1,7},{3,1},{5,3},{7,5},{8,14},{10,8},{12,... | collective-permute-start | bytes 1572872 | tf_op jit(solution)/shard_map/ppermute | solution.py:278
  35.6 0.0 collective-permute-done.4
  35.6 1.8 broadcast_select_fusion.9
  37.4 1.1 broadcast_in_dim.24
  38.5 1.6 fusion.38
  40.1 7.7 %collective-permute-done.2 = bf16[64,4096]{1,0:T(8,128)(2,1)S(1)} collective-permute-done((bf16[64,4096]{1,0:T(8,128)(2,1)S(1)}, bf16[64,4096]{1,0:T(8,128)(2,1)S(1)}, u32[]{:S(2)}, u32[]{:S(2)}) %collective-permute-start.2) | collective-permute-done | bytes 524320 | tf_op jit(solution)/shard_map/ppermute | solution.py:278
  47.8 0.0 collective-permute-done.3
  47.8 1.1 pad_maximum_fusion.4
  48.9 0.0 collective-permute-done.5
  48.9 0.3 broadcast_select_fusion.5
  49.2 2.0 fusion.32
  51.3 1.5 fusion.26
  52.8 0.0 collective-permute-start.6
  52.8 0.2 multiply_reduce_fusion
  53.0 2.7 %collective-permute-done.6 = bf16[128,4096]{1,0:T(8,128)(2,1)S(1)} collective-permute-done((bf16[128,4096]{1,0:T(8,128)(2,1)}, bf16[128,4096]{1,0:T(8,128)(2,1)S(1)}, u32[]{:S(2)}, u32[]{:S(2)}) %collective-permute-start.6) | collective-permute-done | bytes 1048608 | tf_op jit(solution)/shard_map/ppermute | solution.py:282
  55.7 1.4 broadcast_select_fusion.3
  57.1 1.5 fusion.20
  58.6 1.3 dynamic_update_slice.19
  59.9 5.8 %all-to-all-start.1 = ((f32[32,24,256]{2,1,0:T(8,128)}), f32[32,24,256]{2,1,0:T(8,128)S(1)}, u32[]{:S(2)}, u32[]{:S(2)}) async-start(f32[32,24,256]{2,1,0:T(8,128)} %bitcast.9), calls=%async_computation.1 | async-start | bytes 1572864 | tf_op jit(solution)/shard_map/all_to_all | solution.py:273
  65.7 1.3 collective-permute-start.7
  67.0 2.0 collective-permute-start.8
  69.0 20.0 %all-to-all-done.1 = f32[32,24,256]{2,1,0:T(8,128)S(1)} async-done(((f32[32,24,256]{2,1,0:T(8,128)}), f32[32,24,256]{2,1,0:T(8,128)S(1)}, u32[]{:S(2)}, u32[]{:S(2)}) %all-to-all-start.1) | async-done | bytes 786464 | tf_op jit(solution)/shard_map/all_to_all | solution.py:273
  89.0 0.1 reduce_sum.28
  89.0 0.0 collective-permute-done.7
  89.1 1.0 broadcast_in_dim.30
  90.0 5.1 %all-to-all-start.2 = ((f32[32,24,256]{2,1,0:T(8,128)}), f32[32,24,256]{2,1,0:T(8,128)S(1)}, u32[]{:S(2)}, u32[]{:S(2)}) async-start(f32[32,24,256]{2,1,0:T(8,128)} %broadcast_in_dim.30), calls=%async_computation.2 | async-start | bytes 1572864 | tf_op jit(solution)/shard_map/all_to_all | solution.py:273
  95.2 1.3 collective-permute-start.9
  96.4 9.7 %products.2.refs_7_ = f32[512,1024]{1,0:T(8,128)} custom-call(bf16[512,4096]{1,0:T(8,128)(2,1)} %scored_ref.1, bf16[128,4096]{1,0:T(8,128)(2,1)} %copy-done.7, bf16[128,4096]{1,0:T(8,128)(2,1)} %copy-done.8, bf16[128,4096]{1,0:T(8,128)(2,1)} %copy-done.3, bf16[128,4096]{1,0:T(8,128)(2,1)} %copy-done.2, bf16[128,4096]{1,0:T(8,128)(2,1)} %copy-done.4, ...), custom_call_target="tpu_custom_call" | custom-call | flops 4294967296 | bytes 12582912 | tf_op jit(solution)/shard_map/products/pallas_call | solution.py:236
  106.2 3.0 %collective-permute-done.9 = bf16[64,4096]{1,0:T(8,128)(2,1)S(1)} collective-permute-done((bf16[64,4096]{1,0:T(8,128)(2,1)S(1)}, bf16[64,4096]{1,0:T(8,128)(2,1)S(1)}, u32[]{:S(2)}, u32[]{:S(2)}) %collective-permute-start.9) | collective-permute-done | bytes 524320 | tf_op jit(solution)/shard_map/ppermute | solution.py:278
  109.2 1.5 pad_maximum_fusion.2
  110.6 7.3 %all-to-all-done.2 = f32[32,24,256]{2,1,0:T(8,128)S(1)} async-done(((f32[32,24,256]{2,1,0:T(8,128)}), f32[32,24,256]{2,1,0:T(8,128)S(1)}, u32[]{:S(2)}, u32[]{:S(2)}) %all-to-all-start.2) | async-done | bytes 786464 | tf_op jit(solution)/shard_map/all_to_all | solution.py:273
  117.9 0.0 collective-permute-start.13
  117.9 1.2 collective-permute-start.11
  119.1 2.0 collective-permute-start.12
  121.2 0.0 collective-permute-start.10
  121.2 17.9 %collective-permute-done.11.refs_3_ = f32[768,256]{1,0:T(8,128)S(1)} collective-permute-done((f32[768,256]{1,0:T(8,128)S(1)}, f32[768,256]{1,0:T(8,128)S(1)}, u32[]{:S(2)}, u32[]{:S(2)}) %collective-permute-start.11) | collective-permute-done | bytes 786464 | tf_op jit(solution)/shard_map/ppermute | solution.py:278
  139.1 0.0 collective-permute-done.12.refs_2_
  139.1 0.0 collective-permute-done.13
  139.2 0.1 pad_maximum_fusion.3
  139.3 1.5 collective-permute-start.15
  140.8 1.8 collective-permute-start.16
  142.6 0.0 collective-permute-start.14
  142.6 2.5 %broadcast_select_fusion = (bf16[256,4096]{1,0:T(8,128)(2,1)S(1)}, bf16[256,4096]{1,0:T(8,128)(2,1)S(1)}) fusion(bf16[256,4096]{1,0:T(8,128)(2,1)} %collective-permute-done.13, bf16[256,4096]{1,0:T(8,128)(2,1)} %pad_maximum_fusion.2, pred[]{:T(512)S(6)} %eq.11), kind=kLoop, calls=%fused_computation.22 | loop fusion | flops 2097152 | bytes 8388609 | tf_op jit(solution)/shard_map/jit(_where)/select_n | solution.py:345
  145.1 2.3 %pad_maximum_fusion = (bf16[2,128,4096]{2,1,0:T(8,128)(2,1)}, bf16[2,128,4096]{2,1,0:T(8,128)(2,1)}) fusion(bf16[4,64,4096]{2,1,0:T(8,128)(2,1)S(1)} %bitcast.37, bf16[4,64,4096]{2,1,0:T(8,128)(2,1)S(1)} %bitcast.38), kind=kLoop, calls=%fused_computation.3 | loop fusion | flops 8388608 | bytes 8388608 | tf_op jit(solution)/shard_map/concatenate | solution.py:346
  147.4 7.2 %products.3.refs_8_ = f32[512,512]{1,0:T(8,128)} custom-call(bf16[512,4096]{1,0:T(8,128)(2,1)} %scored_ref.1, bf16[256,4096]{1,0:T(8,128)(2,1)} %bitcast.40, bf16[256,4096]{1,0:T(8,128)(2,1)} %bitcast.39), custom_call_target="tpu_custom_call" | custom-call | flops 2147483648 | bytes 8388608 | tf_op jit(solution)/shard_map/products/pallas_call | solution.py:236
  154.5 0.0 collective-permute-done.15
  154.5 1.0 pad_maximum_fusion.5.refs_5_
  155.6 0.8 collective-permute-start.17
  156.4 0.1 pad_add_fusion.place_ref
  156.5 1.8 collective-permute-done.17.refs_6_
  158.3 42.8 %solve.1 = bf16[512,512]{1,0:T(8,128)(2,1)S(1)} custom-call(s32[2]{0:T(128)S(1)} %pad_add_fusion.place_ref, f32[768,256]{1,0:T(8,128)S(1)} %bitcast.35, f32[768,256]{1,0:T(8,128)S(1)} %collective-permute-done.10.refs_1_, f32[768,256]{1,0:T(8,128)S(1)} %collective-permute-done.12.refs_2_, f32[768,256]{1,0:T(8,128)S(1)} %collective-permute-done.11.refs_3_, ...), custom_call_target="tpu_custom_call" | custom-call | flops 20000000000 | bytes 12000000 | tf_op jit(solution)/shard_map/solve/pallas_call | solution.py:251
  201.1 22.9 %all_to_all.34 = bf16[32,16,512]{2,1,0:T(8,128)(2,1)S(1)} all-to-all(bf16[32,16,512]{2,1,0:T(8,128)(2,1)S(1)} %bitcast.36), channel_id=1, replica_groups=mesh['feat_0'=4,'feat_1'=8,'dp_0'=4,'dp_1'=2] {'feat_0','feat_1'}, dimensions={0} | all-to-all | bytes 1048576 | tf_op jit(solution)/shard_map/all_to_all | solution.py:273
  224.0 0.7 convert_reduce_fusion
  (31 shorter events, 0.2 us)
Async XLA Ops:
  0.0 31.9 %collective-permute-start = (bf16[128,4096]{1,0:T(8,128)(2,1)}, bf16[128,4096]{1,0:T(8,128)(2,1)S(1)}, u32[]{:S(2)}, u32[]{:S(2)}) collective-permute-start(bf16[128,4096]{1,0:T(8,128)(2,1)} %param.4), channel_id=1, source_target_pairs={{0,2},{2,4},{4,6},{6,0},{1,3},{3,5},{5,7},{7,1},{8,10},{10,12},{12... | collective-permute-start | bytes 3145736 | tf_op jit(solution)/shard_map/ppermute | solution.py:278
  1.5 30.4 %collective-permute-start.1 = (bf16[128,4096]{1,0:T(8,128)(2,1)}, bf16[128,4096]{1,0:T(8,128)(2,1)S(1)}, u32[]{:S(2)}, u32[]{:S(2)}) collective-permute-start(bf16[128,4096]{1,0:T(8,128)(2,1)} %param.4), channel_id=1, source_target_pairs={{0,6},{2,0},{4,2},{6,4},{1,7},{3,1},{5,3},{7,5},{8,14},{10,8},{12,... | collective-permute-start | bytes 3145736 | tf_op jit(solution)/shard_map/ppermute | solution.py:278
  3.2 28.4 %all-to-all-start = ((bf16[2,32,4096]{2,0,1:T(2,128)(2,1)}), bf16[2,32,4096]{2,0,1:T(2,128)(2,1)S(1)}, u32[]{:S(2)}, u32[]{:S(2)}) async-start(bf16[2,32,4096]{2,0,1:T(2,128)(2,1)} %bitcast.42), calls=%async_computation | async-start | bytes 1048576 | tf_op jit(solution)/shard_map/all_to_all | solution.py:305
  14.6 21.0 %collective-permute-start.4 = (bf16[128,4096]{1,0:T(8,128)(2,1)}, bf16[128,4096]{1,0:T(8,128)(2,1)}, u32[]{:S(2)}, u32[]{:S(2)}) collective-permute-start(bf16[128,4096]{1,0:T(8,128)(2,1)} %param.4), channel_id=1, source_target_pairs={{0,1},{1,0},{2,3},{3,2},{4,5},{5,4},{6,7},{7,6},{8,9},{9,8},{10,11... | collective-permute-start | bytes 3145736 | tf_op jit(solution)/shard_map/ppermute | solution.py:282
  32.0 3.6 %copy-start.6 = (bf16[128,4096]{1,0:T(8,128)(2,1)S(1)}, bf16[128,4096]{1,0:T(8,128)(2,1)}, u32[]{:S(2)}) copy-start(bf16[128,4096]{1,0:T(8,128)(2,1)} %param.4) | copy-start | bytes 3145732
  32.1 16.8 %collective-permute-start.5 = (bf16[256,4096]{1,0:T(8,128)(2,1)S(1)}, bf16[256,4096]{1,0:T(8,128)(2,1)S(1)}, u32[]{:S(2)}, u32[]{:S(2)}) collective-permute-start(bf16[256,4096]{1,0:T(8,128)(2,1)S(1)} %pad_maximum_fusion.1), channel_id=1, source_target_pairs={{0,1},{1,0},{2,3},{3,2},{4,5},{5,4},{6,7},{7,6},{8,9},{9,8},{10,11... | collective-permute-start | bytes 6291464 | tf_op jit(solution)/shard_map/ppermute | solution.py:282
  32.2 15.5 %collective-permute-start.2 = (bf16[64,4096]{1,0:T(8,128)(2,1)S(1)}, bf16[64,4096]{1,0:T(8,128)(2,1)S(1)}, u32[]{:S(2)}, u32[]{:S(2)}) collective-permute-start(bf16[64,4096]{1,0:T(8,128)(2,1)S(1)} %slice.26), channel_id=1, source_target_pairs={{0,2},{2,4},{4,6},{6,0},{1,3},{3,5},{5,7},{7,1},{8,10},{10,12},{12... | collective-permute-start | bytes 1572872 | tf_op jit(solution)/shard_map/ppermute | solution.py:278
  32.6 15.2 %collective-permute-start.3 = (bf16[64,4096]{1,0:T(8,128)(2,1)S(1)}, bf16[64,4096]{1,0:T(8,128)(2,1)S(1)}, u32[]{:S(2)}, u32[]{:S(2)}) collective-permute-start(bf16[64,4096]{1,0:T(8,128)(2,1)S(1)} %slice.27), channel_id=1, source_target_pairs={{0,6},{2,0},{4,2},{6,4},{1,7},{3,1},{5,3},{7,5},{8,14},{10,8},{12,... | collective-permute-start | bytes 1572872 | tf_op jit(solution)/shard_map/ppermute | solution.py:278
  37.3 2.7 %copy-start.7 = (bf16[128,4096]{1,0:T(8,128)(2,1)}, bf16[128,4096]{1,0:T(8,128)(2,1)S(1)}, u32[]{:S(2)}) copy-start(bf16[128,4096]{1,0:T(8,128)(2,1)S(1)} %get-tuple-element.55.refs_0_) | copy-start | bytes 3145732
  37.4 2.7 %copy-start.8 = (bf16[128,4096]{1,0:T(8,128)(2,1)}, bf16[128,4096]{1,0:T(8,128)(2,1)S(1)}, u32[]{:S(2)}) copy-start(bf16[128,4096]{1,0:T(8,128)(2,1)S(1)} %get-tuple-element.56.refs_1_) | copy-start | bytes 3145732
  37.4 13.8 %copy-start.9 = (bf16[192,4096]{1,0:T(8,128)(2,1)}, bf16[192,4096]{1,0:T(8,128)(2,1)S(1)}, u32[]{:S(2)}) copy-start(bf16[192,4096]{1,0:T(8,128)(2,1)S(1)} %constant_dynamic-update-slice_fusion) | copy-start | bytes 4718596
  49.2 2.1 copy-start.2
  49.2 2.1 copy-start.3
  49.2 2.1 copy-start
  49.2 2.1 copy-start.1
  52.8 2.9 %collective-permute-start.6 = (bf16[128,4096]{1,0:T(8,128)(2,1)}, bf16[128,4096]{1,0:T(8,128)(2,1)S(1)}, u32[]{:S(2)}, u32[]{:S(2)}) collective-permute-start(bf16[128,4096]{1,0:T(8,128)(2,1)} %pad_maximum_fusion.4), channel_id=1, source_target_pairs={{0,1},{1,0},{2,3},{3,2},{4,5},{5,4},{6,7},{7,6},{8,9},{9,8},{10,11... | collective-permute-start | bytes 3145736 | tf_op jit(solution)/shard_map/ppermute | solution.py:282
  53.0 4.0 %copy-start.10 = (bf16[192,4096]{1,0:T(8,128)(2,1)S(1)}, bf16[192,4096]{1,0:T(8,128)(2,1)}, u32[]{:S(2)}) copy-start(bf16[192,4096]{1,0:T(8,128)(2,1)} %copy-done.9) | copy-start | bytes 4718596
  57.0 1.6 copy-start.4
  57.0 1.6 copy-start.5
  59.9 29.1 %all-to-all-start.1 = ((f32[32,24,256]{2,1,0:T(8,128)}), f32[32,24,256]{2,1,0:T(8,128)S(1)}, u32[]{:S(2)}, u32[]{:S(2)}) async-start(f32[32,24,256]{2,1,0:T(8,128)} %bitcast.9), calls=%async_computation.1 | async-start | bytes 1572864 | tf_op jit(solution)/shard_map/all_to_all | solution.py:273
  65.7 23.4 %collective-permute-start.7 = (bf16[64,4096]{1,0:T(8,128)(2,1)S(1)}, bf16[64,4096]{1,0:T(8,128)(2,1)S(1)}, u32[]{:S(2)}, u32[]{:S(2)}) collective-permute-start(bf16[64,4096]{1,0:T(8,128)(2,1)S(1)} %all_to_all.26), channel_id=1, source_target_pairs={{0,2},{2,4},{4,6},{6,0},{1,3},{3,5},{5,7},{7,1},{8,10},{10,12},{12... | collective-permute-start | bytes 1572872 | tf_op jit(solution)/shard_map/ppermute | solution.py:278
  67.0 22.1 %collective-permute-start.8 = (bf16[64,4096]{1,0:T(8,128)(2,1)S(1)}, bf16[64,4096]{1,0:T(8,128)(2,1)S(1)}, u32[]{:S(2)}, u32[]{:S(2)}) collective-permute-start(bf16[64,4096]{1,0:T(8,128)(2,1)S(1)} %all_to_all.26), channel_id=1, source_target_pairs={{0,6},{2,0},{4,2},{6,4},{1,7},{3,1},{5,3},{7,5},{8,14},{10,8},{12,... | collective-permute-start | bytes 1572872 | tf_op jit(solution)/shard_map/ppermute | solution.py:278
  90.0 27.9 %all-to-all-start.2 = ((f32[32,24,256]{2,1,0:T(8,128)}), f32[32,24,256]{2,1,0:T(8,128)S(1)}, u32[]{:S(2)}, u32[]{:S(2)}) async-start(f32[32,24,256]{2,1,0:T(8,128)} %broadcast_in_dim.30), calls=%async_computation.2 | async-start | bytes 1572864 | tf_op jit(solution)/shard_map/all_to_all | solution.py:273
  95.2 14.0 %collective-permute-start.9 = (bf16[64,4096]{1,0:T(8,128)(2,1)S(1)}, bf16[64,4096]{1,0:T(8,128)(2,1)S(1)}, u32[]{:S(2)}, u32[]{:S(2)}) collective-permute-start(bf16[64,4096]{1,0:T(8,128)(2,1)S(1)} %collective-permute-done.7), channel_id=1, source_target_pairs={{0,2},{2,4},{4,6},{6,0},{1,3},{3,5},{5,7},{7,1},{8,10},{10,12},{12... | collective-permute-start | bytes 1572872 | tf_op jit(solution)/shard_map/ppermute | solution.py:278
  117.9 21.2 %collective-permute-start.13 = (bf16[256,4096]{1,0:T(8,128)(2,1)}, bf16[256,4096]{1,0:T(8,128)(2,1)}, u32[]{:S(2)}, u32[]{:S(2)}) collective-permute-start(bf16[256,4096]{1,0:T(8,128)(2,1)} %pad_maximum_fusion.2), channel_id=1, source_target_pairs={{0,1},{1,0},{2,3},{3,2},{4,5},{5,4},{6,7},{7,6},{8,9},{9,8},{10,11... | collective-permute-start | bytes 6291464 | tf_op jit(solution)/shard_map/ppermute | solution.py:282
  117.9 21.2 %collective-permute-start.11 = (f32[768,256]{1,0:T(8,128)S(1)}, f32[768,256]{1,0:T(8,128)S(1)}, u32[]{:S(2)}, u32[]{:S(2)}) collective-permute-start(f32[768,256]{1,0:T(8,128)S(1)} %bitcast.32), channel_id=1, source_target_pairs={{0,2},{2,4},{4,6},{6,0},{1,3},{3,5},{5,7},{7,1},{8,10},{10,12},{12... | collective-permute-start | bytes 2359304 | tf_op jit(solution)/shard_map/ppermute | solution.py:278
  119.1 20.0 %collective-permute-start.12 = (f32[768,256]{1,0:T(8,128)S(1)}, f32[768,256]{1,0:T(8,128)S(1)}, u32[]{:S(2)}, u32[]{:S(2)}) collective-permute-start(f32[768,256]{1,0:T(8,128)S(1)} %bitcast.33), channel_id=1, source_target_pairs={{0,6},{2,0},{4,2},{6,4},{1,7},{3,1},{5,3},{7,5},{8,14},{10,8},{12,... | collective-permute-start | bytes 2359304 | tf_op jit(solution)/shard_map/ppermute | solution.py:278
  121.2 35.3 %collective-permute-start.10 = (f32[768,256]{1,0:T(8,128)S(1)}, f32[768,256]{1,0:T(8,128)S(1)}, u32[]{:S(2)}, u32[]{:S(2)}) collective-permute-start(f32[768,256]{1,0:T(8,128)S(1)} %bitcast.34), channel_id=1, source_target_pairs={{0,1},{1,0},{2,3},{3,2},{4,5},{5,4},{6,7},{7,6},{8,9},{9,8},{10,11... | collective-permute-start | bytes 2359304 | tf_op jit(solution)/shard_map/ppermute | solution.py:282
  139.3 15.2 %collective-permute-start.15 = (f32[384,256]{1,0:T(8,128)S(1)}, f32[384,256]{1,0:T(8,128)S(1)}, u32[]{:S(2)}, u32[]{:S(2)}) collective-permute-start(f32[384,256]{1,0:T(8,128)S(1)} %slice.30), channel_id=1, source_target_pairs={{0,2},{2,4},{4,6},{6,0},{1,3},{3,5},{5,7},{7,1},{8,10},{10,12},{12... | collective-permute-start | bytes 1179656 | tf_op jit(solution)/shard_map/ppermute | solution.py:278
  140.8 13.8 %collective-permute-start.16 = (f32[384,256]{1,0:T(8,128)S(1)}, f32[384,256]{1,0:T(8,128)}, u32[]{:S(2)}, u32[]{:S(2)}) collective-permute-start(f32[384,256]{1,0:T(8,128)S(1)} %slice.31), channel_id=1, source_target_pairs={{0,6},{2,0},{4,2},{6,4},{1,7},{3,1},{5,3},{7,5},{8,14},{10,8},{12,... | collective-permute-start | bytes 1179656 | tf_op jit(solution)/shard_map/ppermute | solution.py:278
  142.6 15.7 %collective-permute-start.14 = (f32[1536,256]{1,0:T(8,128)S(1)}, f32[1536,256]{1,0:T(8,128)}, u32[]{:S(2)}, u32[]{:S(2)}) collective-permute-start(f32[1536,256]{1,0:T(8,128)S(1)} %pad_maximum_fusion.3), channel_id=1, source_target_pairs={{0,1},{1,0},{2,3},{3,2},{4,5},{5,4},{6,7},{7,6},{8,9},{9,8},{10,11... | collective-permute-start | bytes 4718600 | tf_op jit(solution)/shard_map/ppermute | solution.py:282
  155.6 2.7 %collective-permute-start.17 = (f32[768,256]{1,0:T(8,128)S(1)}, f32[768,256]{1,0:T(8,128)S(1)}, u32[]{:S(2)}, u32[]{:S(2)}) collective-permute-start(f32[768,256]{1,0:T(8,128)S(1)} %pad_maximum_fusion.5.refs_5_), channel_id=1, source_target_pairs={{0,1},{1,0},{2,3},{3,2},{4,5},{5,4},{6,7},{7,6},{8,9},{9,8},{10,11... | collective-permute-start | bytes 2359304 | tf_op jit(solution)/shard_map/ppermute | solution.py:282
